TPU v7x, 256 devices: a whole 4x4x8 slice. The times are simulated.
256 devices in a mesh: seq: 64 (over x_hi, y, z), tp: 4 (over x_lo, core).
Axes of the slice: x: 4 (x_hi: 2, x_lo: 2; x = x_hi * 2 + x_lo), y: 4, z: 8, core: 2. Of those that a mesh axis runs over, the one named last changes fastest.
Arguments:
- features: bfloat16 [16384, 3, 4096], P('seq', None, 'tp'), may hold values from -6 to 6
- short_taps: float32 [3, 7, 4096], P(None, None, 'tp'), may hold values from -2 to 2
- residue: float32 [16, 4096], P(None, 'tp'), may hold values from -1.5 to 1.5
- decay_rate: float32 [16, 4096], P(None, 'tp'), may hold values from 6.1035157e-06 to 0.05
- w_out: bfloat16 [4096, 4096], P('tp', 'seq'), may hold values from -0.09375 to 0.09375
- cotangent: bfloat16 [16384, 4096], P('seq', 'tp'), may hold values from -16 to 16
Outputs:
- mixed: bfloat16 [16384, 4096], P('seq', 'tp')
- grad_features: bfloat16 [16384, 3, 4096], P('seq', None, 'tp')
- grad_weight: float32 [4096, 4096], P('tp', 'seq')
- grad_taps: float32 [3, 7, 4096], P(None, None, 'tp')
- grad_residue: float32 [16, 4096], P(None, 'tp')
- grad_log_rate: float32 [16, 4096], P(None, 'tp')
All inputs are finite; a program needn't handle non-finite values.
Results may differ from a plain program's by a relative error of at most 0.013.
Values may be sent and summed in bfloat16 or wider, within the bound.
No kernel may reach another device: no remote copies, remote signals or barrier semaphores. Data moves between devices by JAX's collectives and lax.ppermute only.
A program may use at most 128 MiB of HBM per device.

v0:
```python
import jax
import jax.numpy as jnp
from jax import lax
from jax.sharding import PartitionSpec as P


def shifted(array, axis, by):
    devices = lax.axis_size(axis)
    pairs = [(i, i + by) for i in range(devices) if 0 <= i + by < devices]
    return lax.ppermute(array, axis, pairs)


def pair_combine(earlier, later):
    return (earlier[0] * later[0], later[0] * earlier[1] + later[1])


def decay_prefix(values, rate_row):
    channels, length = values.shape
    block_len = min(128, length)
    block_count = length // block_len
    offsets = jnp.arange(block_len, dtype=jnp.float32)
    rising = jnp.exp(rate_row[:, None] * offsets[None, :])
    falling = jnp.exp(-rate_row[:, None] * offsets[None, :])
    shaped = values.reshape(channels, block_count, block_len) * rising[:, None, :]
    triangle = (offsets[:, None] <= offsets[None, :]).astype(jnp.float32)
    summed = jnp.einsum("cqs,st->cqt", shaped, triangle, precision=lax.Precision.HIGHEST)
    inside = summed * falling[:, None, :]
    factor = jnp.broadcast_to(jnp.exp(-rate_row * block_len)[:, None], (channels, block_count))
    _, running = lax.associative_scan(pair_combine, (factor, inside[:, :, -1]), axis=1)
    entering = jnp.concatenate([jnp.zeros((channels, 1), jnp.float32), running[:, :-1]], axis=1)
    carried = entering[:, :, None] * jnp.exp(
        -rate_row[:, None, None] * (offsets[None, None, :] + 1.0)
    )
    return (inside + carried).reshape(channels, length)


def modal_output(signal, rates, coeffs, starts):
    length = signal.shape[1]
    offsets = jnp.arange(length, dtype=jnp.float32)

    def one_mode(running_sum, params):
        rate_row, coeff_row, start_row = params
        states = decay_prefix(signal, rate_row) + start_row[:, None] * jnp.exp(
            -rate_row[:, None] * (offsets[None, :] + 1.0)
        )
        return (running_sum + coeff_row[:, None] * states, states)

    result, states_all = lax.scan(one_mode, jnp.zeros_like(signal), (rates, coeffs, starts))
    return (result, states_all)


def modal_grads(states_all, upstream, rates, coeffs, starts, finals):
    length = upstream.shape[1]
    offsets = jnp.arange(length, dtype=jnp.float32)

    def one_mode(running_sum, params):
        rate_row, coeff_row, start_row, final_row, states = params
        adjoint = jnp.flip(decay_prefix(jnp.flip(upstream, 1), rate_row), 1)
        adjoint = adjoint + final_row[:, None] * jnp.exp(
            -rate_row[:, None] * (length - offsets[None, :])
        )
        previous = jnp.concatenate([start_row[:, None], states[:, :-1]], axis=1)
        sums_pair = (jnp.sum(upstream * states, axis=1), jnp.sum(adjoint * previous, axis=1))
        return (running_sum + coeff_row[:, None] * adjoint, sums_pair)

    result, (alpha_rows, beta_rows) = lax.scan(
        one_mode, jnp.zeros_like(upstream), (rates, coeffs, starts, finals, states_all)
    )
    return (result, alpha_rows, beta_rows)


def coef_grads(alpha_rows, beta_rows, rates, residue):
    scales = jnp.sqrt(-jnp.expm1(-2.0 * rates))
    grad_res = scales * alpha_rows
    grad_log = rates * (
        alpha_rows * residue * jnp.exp(-2.0 * rates) / scales
        - jnp.exp(-rates) * residue * scales * beta_rows
    )
    return (grad_res, grad_log)


def local(features, short_taps, residue, decay_rate, w_out, cotangent):
    tok_count = features.shape[0]
    tap_reach = short_taps.shape[1] - 1
    earlier = shifted(features[tok_count - tap_reach :], "seq", 1)
    extended = jnp.concatenate([earlier, features], axis=0)
    mixed_in = short_taps[:, 0, :] * features
    for tap_index in range(1, tap_reach + 1):
        mixed_in = (
            mixed_in
            + short_taps[:, tap_index, :]
            * extended[tap_reach - tap_index : tap_reach - tap_index + tok_count]
        )
    query_part = mixed_in[:, 0, :]
    keyed = mixed_in[:, 1, :]
    valued = mixed_in[:, 2, :]
    product = (keyed * valued).astype(jnp.bfloat16)
    coeffs = residue * jnp.sqrt(-jnp.expm1(-2.0 * decay_rate))
    mode_count = residue.shape[0]
    chan_share = product.shape[1] // lax.axis_size("seq")
    first_channel = lax.axis_index("seq") * chan_share
    local_rates = lax.dynamic_slice_in_dim(decay_rate, first_channel, chan_share, 1)
    local_coeffs = lax.dynamic_slice_in_dim(coeffs, first_channel, chan_share, 1)
    local_residue = lax.dynamic_slice_in_dim(residue, first_channel, chan_share, 1)
    empty_state = jnp.zeros((mode_count, chan_share), jnp.float32)
    by_channel = lax.all_to_all(product.T, "seq", split_axis=0, concat_axis=1, tiled=True).astype(
        jnp.float32
    )
    conv_channels, mode_states = modal_output(by_channel, local_rates, local_coeffs, empty_state)
    convolved = lax.all_to_all(
        conv_channels.astype(jnp.bfloat16), "seq", split_axis=1, concat_axis=0, tiled=True
    ).T
    gated = (query_part * convolved).astype(jnp.bfloat16)
    full_weight = lax.all_gather(w_out, "seq", axis=1, tiled=True)
    partial_out = jnp.dot(gated, full_weight, preferred_element_type=jnp.float32)
    mixed = lax.psum_scatter(
        partial_out.astype(jnp.bfloat16), "tp", scatter_dimension=1, tiled=True
    )
    grad_rows = lax.all_gather(cotangent, "tp", axis=1, tiled=True)
    grad_gated = lax.dot_general(
        grad_rows, full_weight, (((1,), (1,)), ((), ())), preferred_element_type=jnp.float32
    ).astype(jnp.bfloat16)
    weight_term = lax.dot_general(
        gated, grad_rows, (((0,), (0,)), ((), ())), preferred_element_type=jnp.float32
    )
    grad_weight = lax.psum_scatter(weight_term, "seq", scatter_dimension=1, tiled=True)
    grad_conv = (grad_gated * query_part).astype(jnp.bfloat16)
    grad_channels = lax.all_to_all(
        grad_conv.T, "seq", split_axis=0, concat_axis=1, tiled=True
    ).astype(jnp.float32)
    back_channels, alpha_rows, beta_rows = modal_grads(
        mode_states, grad_channels, local_rates, local_coeffs, empty_state, empty_state
    )
    grad_product = lax.all_to_all(
        back_channels.astype(jnp.bfloat16), "seq", split_axis=1, concat_axis=0, tiled=True
    ).T
    local_res, local_log = coef_grads(alpha_rows, beta_rows, local_rates, local_residue)
    grad_residue, grad_log_rate = (
        lax.all_gather(local_res, "seq", axis=1, tiled=True),
        lax.all_gather(local_log, "seq", axis=1, tiled=True),
    )
    grad_query = grad_gated * convolved
    grad_key = (grad_product * valued).astype(jnp.bfloat16)
    grad_value = (grad_product * keyed).astype(jnp.bfloat16)
    grad_mixed_in = jnp.stack([grad_query, grad_key, grad_value], axis=1)
    later_rows = shifted(grad_mixed_in[:tap_reach], "seq", -1)
    grad_ext = jnp.concatenate([grad_mixed_in, later_rows], axis=0)
    grad_feat = short_taps[:, 0, :] * grad_mixed_in
    tap_terms = [
        jnp.einsum("tjc,tjc->jc", grad_mixed_in, features, preferred_element_type=jnp.float32)
    ]
    for tap_index in range(1, tap_reach + 1):
        grad_feat = (
            grad_feat + short_taps[:, tap_index, :] * grad_ext[tap_index : tap_index + tok_count]
        )
        tap_terms.append(
            jnp.einsum(
                "tjc,tjc->jc",
                grad_mixed_in,
                extended[tap_reach - tap_index : tap_reach - tap_index + tok_count],
                preferred_element_type=jnp.float32,
            )
        )
    tap_local = jnp.stack(tap_terms, axis=1)
    grad_taps = lax.psum(tap_local, "seq")
    return (
        mixed,
        grad_feat.astype(jnp.bfloat16),
        grad_weight,
        grad_taps,
        grad_residue,
        grad_log_rate,
    )


def solution(mesh):
    return jax.shard_map(
        local,
        mesh=mesh,
        in_specs=(
            P("seq", None, "tp"),
            P(None, None, "tp"),
            P(None, "tp"),
            P(None, "tp"),
            P("tp", "seq"),
            P("seq", "tp"),
        ),
        out_specs=(
            P("seq", "tp"),
            P("seq", None, "tp"),
            P("tp", "seq"),
            P(None, None, "tp"),
            P(None, "tp"),
            P(None, "tp"),
        ),
        check_vma=False,
    )
```

profile of v0, /device:TPU:6, one launch (start us, length us, event | category | flops | bytes accessed | tf_op | source)
XLA Modules:
  0.0 2036.1 jit_solution(4164407407298874918)
XLA Ops:
  30.4 13.2 all-gather.5.cloned.1.call-done
  43.6 154.6 %all-gather.3.cloned.1.call-done = bf16[1024,4096]{0,1:T(8,128)(2,1)} async-done(((bf16[1024,64]{0,1:T(8,128)(2,1)}), bf16[1024,4096]{0,1:T(8,128)(2,1)}) %all-gather.3.cloned.1.call-update) | async-done | bytes 8388624 | tf_op jit(solution)/shard_map/all_gather | solution.py:114
  208.0 10.5 all-to-all-start
  221.4 13.4 all-to-all-done
  241.9 183.7 %while.30 = (s32[]{:T(128)}, f32[16,16384]{1,0:T(8,128)}, f32[16,16,16384]{2,1,0:T(8,128)}, f32[16,16]{1,0:T(8,128)S(1)}, f32[16,16384]{1,0:T(8,128)S(1)}, /*ind...) while((s32[]{:T(128)}, f32[16,16384]{1,0:T(8,128)}, ...), condition=%wide.region_1.2_spmd.clone.clone, body=%wide.region_0.1_spmd.clone.clone.sunk | while | flops 406116288 | bytes 18331572 | solution.py:48
  427.7 13.2 all-to-all-start.1
  442.1 509.2 %while.29 = (s32[]{:T(128)}, f32[16,16384]{1,0:T(8,128)}, f32[16,16]{1,0:T(8,128)S(1)}, f32[16,16]{1,0:T(8,128)S(1)}, f32[16,16]{1,0:T(8,128)S(1)}, /*index=5*/f...) while((s32[]{:T(128)}, f32[16,16384]{1,0:T(8,128)}, ...), condition=%wide.region_6.7_spmd.clone, body=%wide.region_3.0_spmd.clone.sunk | while | flops 406378432 | bytes 24557768 | solution.py:66
  461.5 9.2 rev.12
  493.1 9.2 rev.12
  524.9 9.2 rev.12
  556.8 9.2 rev.12
  588.6 9.2 rev.12
  620.4 9.2 rev.12
  652.3 9.2 rev.12
  684.1 9.2 rev.12
  843.3 9.2 rev.12
  953.4 13.3 all-to-all-start.3
  968.8 12.4 all-to-all-done.3
  1000.5 9.9 fusion.47
  1017.0 177.2 %all_gather.14 = f32[16,1024]{0,1:T(8,128)S(1)} all-gather(f32[16,16]{0,1:T(8,128)S(1)} %get-tuple-element.307), channel_id=1, replica_groups=mesh['seq'=64,'tp'=4] {'seq'}, dimensions={1}, use_global_device_ids=true | all-gather | bytes 66560 | tf_op jit(solution)/shard_map/all_gather | solution.py:139
  1195.0 178.3 %all_gather.15 = f32[16,1024]{0,1:T(8,128)S(1)} all-gather(f32[16,16]{0,1:T(8,128)S(1)} %get-tuple-element.306), channel_id=1, replica_groups=mesh['seq'=64,'tp'=4] {'seq'}, dimensions={1}, use_global_device_ids=true | all-gather | bytes 66560 | tf_op jit(solution)/shard_map/all_gather | solution.py:140
  1378.0 219.9 %all-reduce.33.cloned.1.call-done = f32[3,7,1024]{2,0,1:T(4,128)} async-done(((f32[3,7,1024]{2,0,1:T(4,128)}), f32[3,7,1024]{2,0,1:T(4,128)}) %all-reduce.33.cloned.1.call-update) | async-done | bytes 86032 | tf_op jit(solution)/shard_map/psum | solution.py:165
  1599.5 26.1 %reduce-scatter.3.cloned.1.call-done = bf16[256,1024]{1,0:T(8,128)(2,1)} async-done(((bf16[256,4096]{1,0:T(8,128)(2,1)}), bf16[256,1024]{1,0:T(8,128)(2,1)}) %reduce-scatter.3.cloned.1.call-update) | async-done | bytes 524304 | tf_op jit(solution)/shard_map/reduce_scatter | solution.py:116
  1625.6 404.0 %reduce-scatter.5.cloned.1.call-done = f32[1024,64]{0,1:T(8,128)} async-done(((f32[1024,4096]{0,1:T(8,128)}), f32[1024,64]{0,1:T(8,128)}) %reduce-scatter.5.cloned.1.call-update) | async-done | bytes 262160 | tf_op jit(solution)/shard_map/reduce_scatter | solution.py:126
  (2549 shorter events, 685.9 us)
Async XLA Ops:
  7.2 36.4 %all-gather.5.cloned.1.call-start = ((), (), s32[]{:S(2)}) async-start(), calls=%async_computation.8 | async-start | bytes 2621440 | tf_op jit(solution)/shard_map/all_gather | solution.py:119
  7.9 190.3 %all-gather.3.cloned.1.call-start = ((), (), s32[]{:S(2)}) async-start(), calls=%async_computation.6 | async-start | bytes 8519680 | tf_op jit(solution)/shard_map/all_gather | solution.py:114
  9.5 13.1 collective-permute-start
  30.4 174.2 %copy-start = (f32[256,3,1024]{2,0,1:T(8,128)}, f32[256,3,1024]{2,0,1:T(8,128)S(1)}, u32[]{:S(2)}) copy-start(f32[256,3,1024]{2,0,1:T(8,128)S(1)} %multiply_add_fusion.15) | copy-start | bytes 9437188
  204.5 1.4 copy-start.10
  208.0 26.9 %all-to-all-start = ((bf16[64,16,256]{2,1,0:T(8,128)(2,1)}), bf16[64,16,256]{2,1,0:T(8,128)(2,1)S(1)}, u32[]{:S(2)}, u32[]{:S(2)}) async-start(bf16[64,16,256]{2,1,0:T(8,128)(2,1)} %bitcast.18), calls=%async_computation | async-start | bytes 1048576 | tf_op jit(solution)/shard_map/all_to_all | solution.py:106
  234.9 192.8 %all-to-all-start.2 = ((bf16[64,16,256]{2,1,0:T(8,128)(2,1)}), bf16[64,16,256]{2,1,0:T(8,128)(2,1)}, u32[]{:S(2)}, u32[]{:S(2)}) async-start(bf16[64,16,256]{2,1,0:T(8,128)(2,1)} %bitcast.25), calls=%async_computation.3 | async-start | bytes 1048576 | tf_op jit(solution)/shard_map/all_to_all | solution.py:128
  427.7 525.8 %all-to-all-start.1 = ((bf16[16,64,256]{2,0,1:T(8,128)(2,1)}), bf16[16,64,256]{2,0,1:T(8,128)(2,1)}, u32[]{:S(2)}, u32[]{:S(2)}) async-start(bf16[16,64,256]{2,0,1:T(8,128)(2,1)} %bitcast.189), calls=%async_computation.1 | async-start | bytes 1048576 | tf_op jit(solution)/shard_map/all_to_all | solution.py:110
  953.4 32.5 %copy-start.1 = (f32[256,3,1024]{2,0,1:T(8,128)S(1)}, f32[256,3,1024]{2,0,1:T(8,128)}, u32[]{:S(2)}) copy-start(f32[256,3,1024]{2,0,1:T(8,128)} %copy-done) | copy-start | bytes 9437188
  953.4 27.8 %all-to-all-start.3 = ((bf16[16,64,256]{2,0,1:T(8,128)(2,1)}), bf16[16,64,256]{2,0,1:T(8,128)(2,1)}, u32[]{:S(2)}, u32[]{:S(2)}) async-start(bf16[16,64,256]{2,0,1:T(8,128)(2,1)} %bitcast.291), calls=%async_computation.4 | async-start | bytes 1048576 | tf_op jit(solution)/shard_map/all_to_all | solution.py:134
  966.7 631.2 %all-reduce.33.cloned.1.call-start = ((), (), s32[]{:S(2)}) async-start(), calls=%async_computation.10 | async-start | bytes 229376 | tf_op jit(solution)/shard_map/psum | solution.py:165
  986.0 1.8 copy-start.9
  986.0 1.8 copy-start.11
  986.0 2.8 copy-start.8
  987.8 4.2 copy-start.4
  987.8 4.2 copy-start.6
  987.8 0.9 copy-start.2
  992.1 0.6 copy-start.12
  992.8 632.8 %reduce-scatter.3.cloned.1.call-start = ((), (), s32[]{:S(2)}) async-start(), calls=%async_computation.7 | async-start | bytes 2621440 | tf_op jit(solution)/shard_map/reduce_scatter | solution.py:116
  1000.2 1029.3 %reduce-scatter.5.cloned.1.call-start = ((), (), s32[]{:S(2)}) async-start(), calls=%async_computation.9 | async-start | bytes 17039360 | tf_op jit(solution)/shard_map/reduce_scatter | solution.py:126
  1010.4 1.0 copy-start.3
  1010.4 1.2 copy-start.5
  1010.4 1.4 copy-start.7
  1011.9 362.2 %collective-permute-start.1 = (bf16[6,3,1024]{2,0,1:T(8,128)(2,1)S(1)}, bf16[6,3,1024]{2,0,1:T(8,128)(2,1)S(1)}, u32[]{:S(2)}, u32[]{:S(2)}) collective-permute-start(bf16[6,3,1024]{2,0,1:T(8,128)(2,1)S(1)} %slice.600), channel_id=1, source_target_pairs={{4,0},{8,4},{12,8},{16,12},{20,16},{24,20},{28,24},{32,28},{36,32}... | collective-permute-start | bytes 110600 | tf_op jit(solution)/shard_map/ppermute | solution.py:10
Sparse Core Ops, SparseCore 0:
  9.8 33.7 all-gather.4
  47.3 150.7 all-gather.2
  992.9 604.9 all-reduce.32
  1601.0 24.4 reduce-scatter.2
  1628.5 400.9 reduce-scatter.4
where the time goes:
time: 2040 us
  waiting for transfers between devices  853 us (42%)
  local copies, waits for them, and re-layouts  456 us (22%)
  blocking collectives  355 us (17%)
  other arithmetic  252 us (12%)
  starting transfers between devices  53 us (3%)
  matrix products  45.4 us (2%)
    reduce_scatter x1, waiting for transfers between devices, local(): lax.psum_scatter(weight_term, 'seq', scatter_dimension=1, tiled=True)  404 us
    rev x32, local copies, waits for them, and re-layouts, one_mode(): adjoint = jnp.flip(decay_prefix(jnp.flip(upstream, 1), rate_row), 1)  294 us
    psum x1, waiting for transfers between devices, local(): grad_taps = lax.psum(tap_local, 'seq')  220 us
    all_gather x1, blocking collectives, local(): lax.all_gather(local_log, 'seq', axis=1, tiled=True)  178 us
    all_gather x1, blocking collectives, local(): lax.all_gather(local_res, 'seq', axis=1, tiled=True)  177 us
    all_gather x1, waiting for transfers between devices, local(): full_weight = lax.all_gather(w_out, 'seq', axis=1, tiled=True)  155 us
    slice x544, local copies, waits for them, and re-layouts, decay_prefix(): lax.associative_scan(pair_combine, (factor, inside[:, :, -1]), axis=1)  63.4 us
    reduce_sum x16, other arithmetic, one_mode(): jnp.sum(adjoint * previous, axis=1)  48.7 us
  transfers between devices with their start and end apart: 11, of which 8 were waited for; matrix products, arithmetic and copies ran while one was open for 36% of the time, Pallas kernels for 0%

commit v1 on v0

--- a/solution.py
+++ b/solution.py
@@ -162,7 +162,7 @@
             )
         )
     tap_local = jnp.stack(tap_terms, axis=1)
-    grad_taps = lax.psum(tap_local, "seq")
+    grad_taps = jnp.sum(lax.all_gather(tap_local, "seq"), axis=0)
     return (
         mixed,
         grad_feat.astype(jnp.bfloat16),

time: 2040 us -> 1570 us (0.77)
  waiting for transfers between devices: 853 us -> 379 us
    reduce_scatter x1, waiting for transfers between devices: 404 us -> 175 us  [local(): lax.psum_scatter(weight_term, 'seq', scatter_dimension=1, tiled=True)]
    psum x1 -> x0, waiting for transfers between devices: 220 us -> none  [local(): grad_taps = lax.psum(tap_local, 'seq')]
    reduce_scatter x1, waiting for transfers between devices: 26.1 us -> 0.01 us  [local(): lax.psum_scatter(partial_out.astype(jnp.bfloat16), 'tp', scatter_dimensio...]
  transfers between devices with their start and end apart: 11 -> 11, of which waited for: 8 -> 6; matrix products, arithmetic and copies ran while one was open for 36% -> 47% of each run, Pallas kernels for 0% -> 0%
where the time goes in v1:
time: 1570 us
  local copies, waits for them, and re-layouts  454 us (29%)
  waiting for transfers between devices  379 us (24%)
  blocking collectives  357 us (23%)
  other arithmetic  256 us (16%)
  starting transfers between devices  52.9 us (3%)
  matrix products  45.3 us (3%)
    rev x32, local copies, waits for them, and re-layouts, one_mode(): adjoint = jnp.flip(decay_prefix(jnp.flip(upstream, 1), rate_row), 1)  294 us
    all_gather x1, blocking collectives, local(): lax.all_gather(local_log, 'seq', axis=1, tiled=True)  179 us
    all_gather x1, blocking collectives, local(): lax.all_gather(local_res, 'seq', axis=1, tiled=True)  178 us
    reduce_scatter x1, waiting for transfers between devices, local(): lax.psum_scatter(weight_term, 'seq', scatter_dimension=1, tiled=True)  175 us
    all_gather x1, waiting for transfers between devices, local(): full_weight = lax.all_gather(w_out, 'seq', axis=1, tiled=True)  155 us
    slice x544, local copies, waits for them, and re-layouts, decay_prefix(): lax.associative_scan(pair_combine, (factor, inside[:, :, -1]), axis=1)  63.4 us
    reduce_sum x16, other arithmetic, one_mode(): jnp.sum(adjoint * previous, axis=1)  49.2 us
    add x16, other arithmetic, one_mode(): return (running_sum + coeff_row[:, None] * states, states)  45.8 us
  transfers between devices with their start and end apart: 11, of which 6 were waited for; matrix products, arithmetic and copies ran while one was open for 47% of the time, Pallas kernels for 0%

profile of v1, /device:TPU:6, one launch (start us, length us, event | category | flops | bytes accessed | tf_op | source)
XLA Modules:
  0.0 1566.1 jit_solution(13879045894900150003)
XLA Ops:
  30.1 13.5 all-gather.7.cloned.1.call-done
  43.6 154.6 %all-gather.5.cloned.1.call-done = bf16[1024,4096]{0,1:T(8,128)(2,1)} async-done(((bf16[1024,64]{0,1:T(8,128)(2,1)}), bf16[1024,4096]{0,1:T(8,128)(2,1)}) %all-gather.5.cloned.1.call-update) | async-done | bytes 8388624 | tf_op jit(solution)/shard_map/all_gather | solution.py:114
  208.0 10.5 all-to-all-start
  221.4 13.5 all-to-all-done
  241.9 183.7 %while.30 = (s32[]{:T(128)}, f32[16,16384]{1,0:T(8,128)}, f32[16,16,16384]{2,1,0:T(8,128)}, f32[16,16]{1,0:T(8,128)S(1)}, f32[16,16384]{1,0:T(8,128)S(1)}, /*ind...) while((s32[]{:T(128)}, f32[16,16384]{1,0:T(8,128)}, ...), condition=%wide.region_1.2_spmd.clone.clone, body=%wide.region_0.1_spmd.clone.clone.sunk | while | flops 406116288 | bytes 18331572 | solution.py:48
  427.6 13.2 all-to-all-start.1
  442.1 509.6 %while.29 = (s32[]{:T(128)}, f32[16,16384]{1,0:T(8,128)}, f32[16,16]{1,0:T(8,128)S(1)}, f32[16,16]{1,0:T(8,128)S(1)}, f32[16,16]{1,0:T(8,128)S(1)}, /*index=5*/f...) while((s32[]{:T(128)}, f32[16,16384]{1,0:T(8,128)}, ...), condition=%wide.region_6.7_spmd.clone, body=%wide.region_3.0_spmd.clone.sunk | while | flops 406378432 | bytes 24557768 | solution.py:66
  461.5 9.2 rev.12
  493.1 9.2 rev.12
  524.9 9.2 rev.12
  556.8 9.2 rev.12
  588.7 9.2 rev.12
  620.5 9.2 rev.12
  652.4 9.2 rev.12
  684.3 9.2 rev.12
  811.8 9.2 rev.12
  843.6 9.2 rev.12
  907.4 9.2 rev.12
  953.9 13.3 all-to-all-start.3
  969.2 12.5 all-to-all-done.3
  1001.0 9.9 fusion.47
  1017.5 178.3 %all_gather.22 = f32[16,1024]{0,1:T(8,128)S(1)} all-gather(f32[16,16]{0,1:T(8,128)S(1)} %get-tuple-element.295), channel_id=1, replica_groups=mesh['seq'=64,'tp'=4] {'seq'}, dimensions={1}, use_global_device_ids=true | all-gather | bytes 66560 | tf_op jit(solution)/shard_map/all_gather | solution.py:139
  1196.6 178.7 %all_gather.23 = f32[16,1024]{0,1:T(8,128)S(1)} all-gather(f32[16,16]{0,1:T(8,128)S(1)} %get-tuple-element.294), channel_id=1, replica_groups=mesh['seq'=64,'tp'=4] {'seq'}, dimensions={1}, use_global_device_ids=true | all-gather | bytes 66560 | tf_op jit(solution)/shard_map/all_gather | solution.py:140
  1384.2 175.4 %reduce-scatter.5.cloned.1.call-done = f32[1024,64]{0,1:T(8,128)} async-done(((f32[1024,4096]{0,1:T(8,128)}), f32[1024,64]{0,1:T(8,128)}) %reduce-scatter.5.cloned.1.call-update) | async-done | bytes 262160 | tf_op jit(solution)/shard_map/reduce_scatter | solution.py:126
  (2548 shorter events, 670.3 us)
Async XLA Ops:
  7.2 36.4 %all-gather.7.cloned.1.call-start = ((), (), s32[]{:S(2)}) async-start(), calls=%async_computation.8 | async-start | bytes 2621440 | tf_op jit(solution)/shard_map/all_gather | solution.py:119
  7.9 190.3 %all-gather.5.cloned.1.call-start = ((), (), s32[]{:S(2)}) async-start(), calls=%async_computation.6 | async-start | bytes 8519680 | tf_op jit(solution)/shard_map/all_gather | solution.py:114
  9.5 13.1 collective-permute-start
  30.1 174.4 %copy-start = (f32[256,3,1024]{2,0,1:T(8,128)}, f32[256,3,1024]{2,0,1:T(8,128)S(1)}, u32[]{:S(2)}) copy-start(f32[256,3,1024]{2,0,1:T(8,128)S(1)} %multiply_add_fusion.15) | copy-start | bytes 9437188
  204.5 1.4 copy-start.10
  208.0 26.9 %all-to-all-start = ((bf16[64,16,256]{2,1,0:T(8,128)(2,1)}), bf16[64,16,256]{2,1,0:T(8,128)(2,1)S(1)}, u32[]{:S(2)}, u32[]{:S(2)}) async-start(bf16[64,16,256]{2,1,0:T(8,128)(2,1)} %bitcast.18), calls=%async_computation | async-start | bytes 1048576 | tf_op jit(solution)/shard_map/all_to_all | solution.py:106
  234.9 192.7 %all-to-all-start.2 = ((bf16[64,16,256]{2,1,0:T(8,128)(2,1)}), bf16[64,16,256]{2,1,0:T(8,128)(2,1)}, u32[]{:S(2)}, u32[]{:S(2)}) async-start(bf16[64,16,256]{2,1,0:T(8,128)(2,1)} %bitcast.25), calls=%async_computation.3 | async-start | bytes 1048576 | tf_op jit(solution)/shard_map/all_to_all | solution.py:128
  427.6 526.2 %all-to-all-start.1 = ((bf16[16,64,256]{2,0,1:T(8,128)(2,1)}), bf16[16,64,256]{2,0,1:T(8,128)(2,1)}, u32[]{:S(2)}, u32[]{:S(2)}) async-start(bf16[16,64,256]{2,0,1:T(8,128)(2,1)} %bitcast.176), calls=%async_computation.1 | async-start | bytes 1048576 | tf_op jit(solution)/shard_map/all_to_all | solution.py:110
  953.8 32.6 %copy-start.1 = (f32[256,3,1024]{2,0,1:T(8,128)S(1)}, f32[256,3,1024]{2,0,1:T(8,128)}, u32[]{:S(2)}) copy-start(f32[256,3,1024]{2,0,1:T(8,128)} %copy-done) | copy-start | bytes 9437188
  953.9 27.8 %all-to-all-start.3 = ((bf16[16,64,256]{2,0,1:T(8,128)(2,1)}), bf16[16,64,256]{2,0,1:T(8,128)(2,1)}, u32[]{:S(2)}, u32[]{:S(2)}) async-start(bf16[16,64,256]{2,0,1:T(8,128)(2,1)} %bitcast.279), calls=%async_computation.4 | async-start | bytes 1048576 | tf_op jit(solution)/shard_map/all_to_all | solution.py:134
  967.1 412.9 %all-gather.9.cloned.1.call-start = ((), (), s32[]{:S(2)}) async-start(), calls=%async_computation.10 | async-start | bytes 6389760 | tf_op jit(solution)/shard_map/all_gather | solution.py:165
  986.4 1.8 copy-start.9
  986.4 1.8 copy-start.11
  986.4 2.8 copy-start.8
  988.2 4.2 copy-start.4
  988.2 4.2 copy-start.6
  988.3 0.9 copy-start.2
  993.4 390.8 %reduce-scatter.3.cloned.1.call-start = ((), (), s32[]{:S(2)}) async-start(), calls=%async_computation.7 | async-start | bytes 2621440 | tf_op jit(solution)/shard_map/reduce_scatter | solution.py:116
  1000.7 558.9 %reduce-scatter.5.cloned.1.call-start = ((), (), s32[]{:S(2)}) async-start(), calls=%async_computation.9 | async-start | bytes 17039360 | tf_op jit(solution)/shard_map/reduce_scatter | solution.py:126
  1010.9 1.0 copy-start.3
  1010.9 1.2 copy-start.5
  1010.9 1.4 copy-start.7
  1012.4 363.7 %collective-permute-start.1 = (bf16[6,3,1024]{2,0,1:T(8,128)(2,1)S(1)}, bf16[6,3,1024]{2,0,1:T(8,128)(2,1)S(1)}, u32[]{:S(2)}, u32[]{:S(2)}) collective-permute-start(bf16[6,3,1024]{2,0,1:T(8,128)(2,1)S(1)} %slice.600), channel_id=1, source_target_pairs={{4,0},{8,4},{12,8},{16,12},{20,16},{24,20},{28,24},{32,28},{36,32}... | collective-permute-start | bytes 110600 | tf_op jit(solution)/shard_map/ppermute | solution.py:10
Sparse Core Ops, SparseCore 0:
  9.8 33.7 all-gather.6
  47.3 150.7 all-gather.4
  993.5 133.0 all-gather.8
  1129.5 27.1 reduce-scatter.2
  1159.9 399.6 reduce-scatter.4
